TPU v7x, 32 devices: a whole 2x2x4 slice. The times are simulated.
32 devices in a mesh: sec: 2 (over core), row: 4 (over y, x), col: 4 (over z).
Axes of the slice: x: 2, y: 2, z: 4, core: 2. Of those that a mesh axis runs over, the one named last changes fastest.
Arguments:
- anc_inverse: float32 [2048, 2048], P('row', ('sec', 'col')), as said below
- panel: float32 [8192, 2048], P(('sec', 'col'), 'row'), may hold values from -0.5 to 0.5
- diag_inverse: float32 [8192, 512], P(('sec', 'col')), may hold values from -6 to 6
- widths: int32 [16], replicated, may hold values from 1 to 4, as said below
- pattern: int32 [16, 16], replicated, may hold values 0 or 1
Outputs:
- off_inverse: float32 [8192, 2048], P(('sec', 'col'), 'row')
- child_inverse: float32 [8192, 512], P(('sec', 'col'))
Inputs may be any that keep to these rules, and one draw needn't show every extreme that they name: `anc_inverse`: exactly symmetric. `widths`: both 1 and 4 occur in every draw.
All inputs are finite; a program needn't handle non-finite values.
Results may differ from a plain program's by a relative error of at most 0.0003.
Values sent between devices are 32-bit elements; how exact they have to be, the bound alone decides.
A program may use at most 128 MiB of HBM per device.

v0:
```python
import jax
import jax.numpy as jnp
from jax import lax
from jax.sharding import PartitionSpec as P

B = 128
SW = 512


def mask_rows(values, slot_count, column_mask, block_mask, offset):
    amount = values.shape[1]
    window = lax.dynamic_slice_in_dim(block_mask, offset, amount, 1)
    shaped = (
        values.reshape(slot_count, SW, amount)
        * column_mask.reshape(slot_count, SW, 1)
        * window[:, None, :]
    )
    return shaped.reshape(slot_count * SW, amount)


def local(anc_inverse, panel, diag_inverse, widths, pattern):
    highest = lax.Precision.HIGHEST
    local_rows, rows_here = panel.shape
    slot_count = local_rows // SW
    slot_first = (lax.axis_index("sec") * lax.axis_size("col") + lax.axis_index("col")) * slot_count
    row_offset = lax.axis_index("row") * rows_here
    my_widths = lax.dynamic_slice_in_dim(widths, slot_first, slot_count)
    my_pattern = lax.dynamic_slice_in_dim(pattern, slot_first, slot_count, 0)
    block_mask = jnp.repeat(my_pattern.astype(jnp.float32), B, axis=1)
    position = jnp.arange(SW, dtype=jnp.int32)
    column_mask = (position[None, :] < my_widths[:, None] * B).astype(jnp.float32)
    anc_rows = lax.all_gather(anc_inverse, ("sec", "col"), axis=1, tiled=True)
    local_panel = mask_rows(panel, slot_count, column_mask, block_mask, row_offset)
    product = lax.psum_scatter(
        lax.dot_general(
            anc_rows,
            local_panel,
            (((0,), (1,)), ((), ())),
            precision=highest,
            preferred_element_type=jnp.float32,
        ),
        "row",
        scatter_dimension=0,
        tiled=True,
    ).T
    product = mask_rows(product, slot_count, column_mask, block_mask, row_offset)
    update = jnp.einsum(
        "jai,jbi->jab",
        product.reshape(slot_count, SW, rows_here),
        local_panel.reshape(slot_count, SW, rows_here),
        precision=highest,
    )
    summed = lax.psum(update.reshape(local_rows, SW), "row")
    pair_mask = column_mask[:, :, None] * column_mask[:, None, :]
    diag_block = (diag_inverse + summed) * pair_mask.reshape(local_rows, SW)
    return (-product, diag_block)


def solution(mesh):
    in_specs = (
        P("row", ("sec", "col")),
        P(("sec", "col"), "row"),
        P(("sec", "col"), None),
        P(),
        P(),
    )
    out_specs = (P(("sec", "col"), "row"), P(("sec", "col"), None))
    return jax.shard_map(local, mesh=mesh, in_specs=in_specs, out_specs=out_specs, check_vma=False)
```

profile of v0, /device:TPU:0, one launch (start us, length us, event | category | flops | bytes accessed | tf_op | source)
XLA Modules:
  0.0 249.4 jit_solution(4259381773065099106)
XLA Ops:
  7.2 0.0 all-gather.2.cloned.1.call-start
  7.2 0.7 all-gather.2.cloned.1.call-update
  7.9 0.0 reduce-scatter.2.cloned.1.call-start
  8.0 0.7 dynamic-slice_multiply_fusion
  8.7 0.1 compare_convert_fusion
  8.8 0.7 dynamic-slice_convert_fusion
  9.5 0.1 broadcast_bitcast_fusion
  9.6 1.8 bitcast_multiply_fusion.1
  11.4 47.8 %all-gather.2.cloned.1.call-done = f32[512,2048]{1,0:T(8,128)} async-done(((f32[512,256]{1,0:T(8,128)}), f32[512,2048]{1,0:T(8,128)}) %all-gather.2.cloned.1.call-update) | async-done | bytes 4194320 | tf_op jit(solution)/shard_map/all_gather | solution.py:32
  59.2 17.3 %convolution_bitcast_fusion = f32[2048,1024]{0,1:T(8,128)} fusion(f32[1024,512]{1,0:T(8,128)S(1)} %bitcast_multiply_fusion.1, f32[512,2048]{1,0:T(8,128)} %all-gather.2.cloned.1.call-done), kind=kOutput, calls=%fused_computation | convolution fusion | flops 12884901888 | bytes 14680064 | tf_op jit(solution)/shard_map/dot_general | solution.py:35
  76.5 0.0 copy-start
  76.5 0.0 reduce-scatter.2.cloned.1.call-update
  76.5 0.0 all-reduce.2.cloned.1.call-start
  76.6 85.2 %reduce-scatter.2.cloned.1.call-done = f32[512,1024]{0,1:T(8,128)} async-done(((f32[2048,1024]{0,1:T(8,128)}), f32[512,1024]{0,1:T(8,128)}) %reduce-scatter.2.cloned.1.call-update) | async-done | bytes 2097168 | tf_op jit(solution)/shard_map/reduce_scatter | solution.py:34
  161.8 0.0 copy-done
  161.8 6.7 %fusion.2 = f32[2,512,512]{2,1,0:T(8,128)} fusion(f32[2,512,512]{2,1,0:T(8,128)S(1)} %bitcast.29, f32[2,512,512]{2,1,0:T(8,128)} %bitcast.31, f32[2,512]{1,0:T(2,128)S(1)} %get-tuple-element.4, f32[2,512]{1,0:T(2,128)S(1)} %constant_dynamic-slice_fusion), kind=kOutput, calls=%fused_computation.7 | convolution fusion | flops 3223322624 | bytes 6299648 | tf_op jit(solution)/shard_map/jai,jbi->jab/dot_general | solution.py:47
  168.5 0.0 copy-start.1
  168.5 0.0 all-reduce.2.cloned.1.call-update
  168.6 69.7 %all-reduce.2.cloned.1.call-done = f32[1024,512]{1,0:T(8,128)} async-done(((f32[1024,512]{1,0:T(8,128)}), f32[1024,512]{1,0:T(8,128)}) %all-reduce.2.cloned.1.call-update) | async-done | bytes 2097168 | tf_op jit(solution)/shard_map/psum | solution.py:53
  238.2 0.0 copy-done.1
  238.2 4.7 %fusion.1 = (f32[1024,512]{1,0:T(8,128)}, f32[1024,512]{1,0:T(8,128)}) fusion(f32[1024,512]{1,0:T(8,128)} %param.7, f32[1024,512]{1,0:T(8,128)} %all-reduce.2.cloned.1.call-done, f32[2,512]{1,0:T(2,128)S(1)} %get-tuple-element.4, f32[1024]{0:T(1024)S(1)} %bitcast.33, f32[2,512]{1,0:T(2,128)S(1)} %constant_dynamic-slice_fusion, f32[512,1024]{0,1:T(8,128)S(1)} %copy-done.1), kind=kLoop, calls=%fused_computation.5 | loop fusion | flops 3145728 | bytes 10498048 | tf_op jit(solution)/shard_map/mul | solution.py:55
  (3 shorter events, 0.0 us)
Async XLA Ops:
  7.2 52.0 %all-gather.2.cloned.1.call-start = ((), (), s32[]{:S(2)}) async-start(), calls=%async_computation.1 | async-start | bytes 4718592 | tf_op jit(solution)/shard_map/all_gather | solution.py:32
  7.9 153.9 %reduce-scatter.2.cloned.1.call-start = ((), (), s32[]{:S(2)}) async-start(), calls=%async_computation.2 | async-start | bytes 10485760 | tf_op jit(solution)/shard_map/reduce_scatter | solution.py:34
  76.5 85.3 %copy-start = (f32[1024,512]{1,0:T(8,128)S(1)}, f32[1024,512]{1,0:T(8,128)}, u32[]{:S(2)}) copy-start(f32[1024,512]{1,0:T(8,128)} %param.6) | copy-start | bytes 6291460
  76.5 161.7 %all-reduce.2.cloned.1.call-start = ((), (), s32[]{:S(2)}) async-start(), calls=%async_computation.3 | async-start | bytes 4194304 | tf_op jit(solution)/shard_map/psum | solution.py:53
  168.5 69.7 %copy-start.1 = (f32[512,1024]{0,1:T(8,128)S(1)}, f32[512,1024]{0,1:T(8,128)}, u32[]{:S(2)}) copy-start(f32[512,1024]{0,1:T(8,128)} %reduce-scatter.2.cloned.1.call-done) | copy-start | bytes 6291460
Sparse Core Ops, SparseCore 0:
  9.6 49.5 all-gather.1
  76.6 85.1 reduce-scatter.1
  168.7 69.4 all-reduce.1
where the time goes:
time: 250 us; the launch traced here: 249 us
  waiting for transfers between devices  203 us (81%)
  matrix products  24 us (10%)
  between operations  13.8 us (6%)
  other arithmetic  8.03 us (3%)
    reduce_scatter x1, waiting for transfers between devices, local(): lax.psum_scatter(lax.dot_general(anc_rows, local_panel, (((0,), (1,)), ((...  85.2 us
    psum x1, waiting for transfers between devices, local(): summed = lax.psum(update.reshape(local_rows, SW), 'row')  69.7 us
    all_gather x1, waiting for transfers between devices, local(): anc_rows = lax.all_gather(anc_inverse, ('sec', 'col'), axis=1, tiled=True)  47.8 us
    dot_general x1, matrix products, local(): lax.dot_general(anc_rows, local_panel, (((0,), (1,)), ((), ())), precisio...  17.3 us
    dot_general x1, matrix products, local(): jnp.einsum('jai,jbi->jab', product.reshape(slot_count, SW, rows_here), lo...  6.73 us
  transfers between devices with their start and end apart: 3, of which 3 were waited for; matrix products, arithmetic and copies ran while one was open for 1% of the time, Pallas kernels for 0%

commit v1 on v0

v1 whole, which is shorter than its diff:
```python
import functools
import jax
import jax.numpy as jnp
from jax import lax
from jax.experimental import pallas as pl
from jax.experimental.pallas import tpu as pltpu
from jax.sharding import PartitionSpec as P

B = 128
SW = 512
F32 = jnp.float32
BF = jnp.bfloat16
MESH = pl.DeviceIdType.MESH
NN = (((1,), (0,)), ((), ()))
NT = (((1,), (1,)), ((), ()))


def split(value):
    high = value.astype(BF)
    return high, (value - high.astype(F32)).astype(BF)


def dot3(ah, al, bh, bl, dims):
    dot = functools.partial(lax.dot_general, dimension_numbers=dims, preferred_element_type=F32)
    return dot(ah, bh) + (dot(ah, bl) + dot(al, bh))


def factor(count):
    low = 1
    for value in range(1, count + 1):
        if count % value == 0 and value * value <= count:
            low = value
    return count // low, low


def kernel(
    sizes,
    anc_ref, panel_ref, prod_ref, upd_ref,
    anc, ah, al, ph, plo, pin, opp, oh, ol, qsend, qrecv, upack, urecv, usum, ugat,
    zs, zr, ps, pr, os_, or_, qs, qr, us, ur, gs, gr,
):
    nsec, nrow, ncol, nf, ns, nb, square = sizes
    rows, width = panel_ref.shape
    pw = anc_ref.shape[1]
    per = width // pw
    slots = rows // SW
    wb = SW // B
    tri = wb * (wb + 1) // 2
    part = tri * B // nrow
    tm = 256
    sec, row, col = lax.axis_index("sec"), lax.axis_index("row"), lax.axis_index("col")
    turn = sec if square else 0
    a, b = row // nb, row % nb
    f = a + turn * (b - a)
    s = b + turn * (a - b)
    cf = nb - turn * (nb - 1)
    cs = 1 + turn * (nb - 1)

    def at(fi, si):
        return fi * cf + si * cs

    def copy(src, dst, send, recv, where):
        return pltpu.make_async_remote_copy(
            src_ref=src, dst_ref=dst, send_sem=send, recv_sem=recv, device_id=where, device_id_type=MESH
        )

    has_left = (col > 0).astype(jnp.int32)
    has_right = (col < ncol - 1).astype(jnp.int32)
    barrier = pltpu.get_barrier_semaphore()
    for d in range(1, nrow):
        pl.semaphore_signal(barrier, inc=1, device_id={"row": (row + d) % nrow}, device_id_type=MESH)
    pl.semaphore_signal(barrier, inc=1, device_id={"sec": 1 - sec}, device_id_type=MESH)

    @pl.when(col > 0)
    def _():
        pl.semaphore_signal(barrier, inc=1, device_id={"col": col - 1}, device_id_type=MESH)

    @pl.when(col < ncol - 1)
    def _():
        pl.semaphore_signal(barrier, inc=1, device_id={"col": col + 1}, device_id_type=MESH)

    pl.semaphore_wait(barrier, nrow + has_left + has_right)

    mine = sec * ncol + col

    def piece_copy(src, p, way):
        where = ({"col": col - 1}, {"col": col + 1}, {"sec": 1 - sec})[way]
        return copy(src, anc.at[p], zs.at[p, way], zr.at[p], where)

    def opp_copy(src, d, e, k):
        return copy(
            src, opp.at[d - 1, e - 1, k], os_.at[d - 1, e - 1, k], or_.at[d - 1, e - 1, k],
            {"row": at((f + d) % nf, s)},
        )

    def pass_on(src, p):
        for d in range(1, nf):
            for e in range(1, ns):
                @pl.when(p // per == at((f + d) % nf, (s + e) % ns))
                def _():
                    opp_copy(src, d, e, p % per).start()

    def panel_copy(d, j):
        return copy(
            panel_ref.at[pl.ds(j * SW, SW)], pin.at[d - 1, j], ps.at[d - 1, j], pr.at[d - 1, j],
            {"row": at((f + d) % nf, s)},
        )

    def halves(src, p):
        high, low = split(src[...])
        ah[p] = high
        al[p] = low

    @pl.when(col > 0)
    def _():
        piece_copy(anc_ref, mine, 0).start()

    @pl.when(col < ncol - 1)
    def _():
        piece_copy(anc_ref, mine, 1).start()

    piece_copy(anc_ref, mine, 2).start()
    pass_on(anc_ref, mine)
    for j in range(slots):
        for d in range(1, nf):
            panel_copy(d, j).start()

    halves(anc_ref, mine)
    high, low = split(panel_ref[...])
    ph[0] = high
    plo[0] = low

    def from_left(t):
        p = mine - t
        piece_copy(anc_ref, p, 2).wait_recv()

        @pl.when(col < ncol - 1)
        def _():
            piece_copy(anc.at[p], p, 1).start()

        piece_copy(anc.at[p], p, 2).start()
        pass_on(anc.at[p], p)
        halves(anc.at[p], p)

    def from_right(t):
        p = mine + t
        piece_copy(anc_ref, p, 2).wait_recv()

        @pl.when(col > 0)
        def _():
            piece_copy(anc.at[p], p, 0).start()

        piece_copy(anc.at[p], p, 2).start()
        pass_on(anc.at[p], p)
        halves(anc.at[p], p)

    def from_partner(p):
        piece_copy(anc_ref, p, 2).wait_recv()
        pass_on(anc.at[p], p)
        halves(anc.at[p], p)

    other = (1 - sec) * ncol + col
    from_partner(other)

    def gather_step(t, carry):
        pl.when(col - t >= 0)(lambda: from_left(t))
        pl.when(col + t < ncol)(lambda: from_right(t))
        pl.when(col - t >= 0)(lambda: from_partner(other - t))
        pl.when(col + t < ncol)(lambda: from_partner(other + t))
        return carry

    lax.fori_loop(1, ncol, gather_step, 0)

    for j in range(slots):
        for d in range(1, nf):
            panel_copy(d, j).wait_recv()
            high, low = split(pin[d - 1, j])
            ph[d, pl.ds(j * SW, SW)] = high
            plo[d, pl.ds(j * SW, SW)] = low
    for d in range(1, nf):
        for e in range(1, ns):
            for k in range(per):
                opp_copy(anc_ref, d, e, k).wait_recv()
                high, low = split(opp[d - 1, e - 1, k])
                oh[d - 1, e - 1, k] = high
                ol[d - 1, e - 1, k] = low

    def q_copy(e, j):
        return copy(
            qsend.at[e - 1, j], qrecv.at[e - 1, j], qs.at[e - 1, j], qr.at[e - 1, j],
            {"row": at(f, (s + e) % ns)},
        )

    for j in range(slots):
        for e in range(1, ns):
            base = at(f, (s + e) % ns) * per

            def target(i, carry):
                r = pl.multiple_of(i * tm, tm)
                rr = pl.ds(pl.multiple_of(j * SW + r, tm), tm)
                for k in range(per):
                    acc = dot3(ph[0, rr], plo[0, rr], ah[base + k], al[base + k], NN)
                    for d in range(1, nf):
                        acc += dot3(ph[d, rr], plo[d, rr], oh[d - 1, e - 1, k], ol[d - 1, e - 1, k], NN)
                    qsend[e - 1, j, pl.ds(r, tm), pl.ds(k * pw, pw)] = acc
                return carry

            lax.fori_loop(0, SW // tm, target, 0)
            q_copy(e, j).start()

    def own(i, carry):
        rr = pl.ds(pl.multiple_of(i * tm, tm), tm)
        for k in range(per):
            p = at(f, s) * per + k
            prod_ref[rr, pl.ds(k * pw, pw)] = dot3(ph[0, rr], plo[0, rr], ah[p], al[p], NN)
        for d in range(1, nf):
            for k in range(per):
                p = at((f + nf - d) % nf, s) * per + k
                cols = pl.ds(k * pw, pw)
                prod_ref[rr] += dot3(ph[d, rr, cols], plo[d, rr, cols], ah[p], al[p], NT)
        return carry

    lax.fori_loop(0, rows // tm, own, 0)

    def u_copy(j, d):
        return copy(
            upack.at[j, pl.ds(pl.multiple_of(((row + d) % nrow) * part, 8), part)],
            urecv.at[j, d - 1], us.at[j, d - 1], ur.at[j, d - 1], {"row": (row + d) % nrow},
        )

    def g_copy(j, d):
        return copy(
            usum.at[j], ugat.at[j, d - 1], gs.at[j, d - 1], gr.at[j, d - 1], {"row": (row + d) % nrow}
        )

    for j in range(slots):
        jr = pl.ds(j * SW, SW)
        for e in range(1, ns):
            q_copy(e, j).wait_recv()
            prod_ref[jr] += qrecv[e - 1, j]
        spot = 0
        for i in range(wb):
            qh, ql = split(prod_ref[pl.ds(j * SW + i * B, B)])
            rest = pl.ds(j * SW + i * B, SW - i * B)
            line = dot3(qh, ql, ph[0, rest], plo[0, rest], NT)
            for k in range(i, wb):
                upack[j, pl.ds(spot * B, B)] = line[:, (k - i) * B:(k - i + 1) * B]
                spot += 1
        for d in range(1, nrow):
            u_copy(j, d).start()

    for j in range(slots):
        for d in range(1, nrow):
            u_copy(j, d).wait_recv()
        total = upack[j, pl.ds(pl.multiple_of(row * part, 8), part)]
        for d in range(1, nrow):
            total += urecv[j, d - 1]
        usum[j] = total
        for d in range(1, nrow):
            g_copy(j, d).start()

    for j in range(slots):
        for d in range(1, nrow):
            u_copy(j, d).wait_send()
        upack[j, pl.ds(pl.multiple_of(row * part, 8), part)] = usum[j]
        for d in range(1, nrow):
            g_copy(j, d).wait_recv()
            upack[j, pl.ds(pl.multiple_of(((row + nrow - d) % nrow) * part, 8), part)] = ugat[j, d - 1]
        spot = 0
        for i in range(wb):
            for k in range(i, wb):
                block = upack[j, pl.ds(spot * B, B)]
                upd_ref[pl.ds(j * SW + i * B, B), pl.ds(k * B, B)] = block
                if k > i:
                    upd_ref[pl.ds(j * SW + k * B, B), pl.ds(i * B, B)] = block.T
                spot += 1

    for j in range(slots):
        for d in range(1, nrow):
            g_copy(j, d).wait_send()
        for e in range(1, ns):
            q_copy(e, j).wait_send()
        for d in range(1, nf):
            panel_copy(d, j).wait_send()
    for d in range(1, nf):
        for e in range(1, ns):
            for k in range(per):
                opp_copy(anc_ref, d, e, k).wait_send()

    def drain(q, carry):
        p = sec * ncol + q
        pl.when(jnp.logical_and(q <= col, col < ncol - 1))(lambda: piece_copy(anc_ref, p, 1).wait_send())
        pl.when(jnp.logical_and(q >= col, col > 0))(lambda: piece_copy(anc_ref, p, 0).wait_send())
        piece_copy(anc_ref, p, 2).wait_send()
        return carry

    lax.fori_loop(0, ncol, drain, 0)


def exchange(sizes, anc_inverse, panel):
    nsec, nrow, ncol, nf, ns, nb, square = sizes
    rows, width = panel.shape
    pw = anc_inverse.shape[1]
    per = width // pw
    slots = rows // SW
    pieces = nsec * ncol
    wb = SW // B
    packed = wb * (wb + 1) // 2 * B
    part = packed // nrow
    vm = pltpu.VMEM
    dma = pltpu.SemaphoreType.DMA
    whole = pl.BlockSpec(memory_space=pltpu.VMEM)
    return pl.pallas_call(
        functools.partial(kernel, sizes),
        out_shape=(jax.ShapeDtypeStruct((rows, width), F32), jax.ShapeDtypeStruct((rows, SW), F32)),
        in_specs=[whole, whole],
        out_specs=(whole, whole),
        scratch_shapes=[
            vm((pieces, width, pw), F32),
            vm((pieces, width, pw), BF),
            vm((pieces, width, pw), BF),
            vm((nf, rows, width), BF),
            vm((nf, rows, width), BF),
            vm((nf - 1, slots, SW, width), F32),
            vm((nf - 1, ns - 1, per, width, pw), F32),
            vm((nf - 1, ns - 1, per, width, pw), BF),
            vm((nf - 1, ns - 1, per, width, pw), BF),
            vm((ns - 1, slots, SW, width), F32),
            vm((ns - 1, slots, SW, width), F32),
            vm((slots, packed, B), F32),
            vm((slots, nrow - 1, part, B), F32),
            vm((slots, part, B), F32),
            vm((slots, nrow - 1, part, B), F32),
            dma((pieces, 3)), dma((pieces,)),
            dma((nf - 1, slots)), dma((nf - 1, slots)),
            dma((nf - 1, ns - 1, per)), dma((nf - 1, ns - 1, per)),
            dma((ns - 1, slots)), dma((ns - 1, slots)),
            dma((slots, nrow - 1)), dma((slots, nrow - 1)),
            dma((slots, nrow - 1)), dma((slots, nrow - 1)),
        ],
        compiler_params=pltpu.CompilerParams(
            collective_id=0, has_side_effects=True, vmem_limit_bytes=60 * 1024 * 1024
        ),
    )(anc_inverse, panel)


def local(sizes, anc_inverse, panel, diag_inverse, widths, pattern):
    local_rows, rows_here = panel.shape
    slot_count = local_rows // SW
    slot_first = (lax.axis_index("sec") * lax.axis_size("col") + lax.axis_index("col")) * slot_count
    blocks = rows_here // B
    my_widths = lax.dynamic_slice_in_dim(widths, slot_first, slot_count)
    my_pattern = lax.dynamic_slice(
        pattern, (slot_first, lax.axis_index("row") * blocks), (slot_count, blocks)
    )
    block_mask = jnp.repeat(my_pattern.astype(F32), B, axis=1)
    position = jnp.arange(SW, dtype=jnp.int32)
    column_mask = (position[None, :] < my_widths[:, None] * B).astype(F32)
    mask = column_mask[:, :, None] * block_mask[:, None, :]
    masked = (panel.reshape(slot_count, SW, rows_here) * mask).reshape(local_rows, rows_here)
    product, update = exchange(sizes, anc_inverse, masked)
    product = product.reshape(slot_count, SW, rows_here) * mask
    pair_mask = column_mask[:, :, None] * column_mask[:, None, :]
    diag_block = (diag_inverse + update) * pair_mask.reshape(local_rows, SW)
    return (-product.reshape(local_rows, rows_here), diag_block)


def solution(mesh):
    shape = dict(mesh.shape)
    na, nb = factor(shape["row"])
    sizes = (shape["sec"], shape["row"], shape["col"], na, nb, nb, na == nb)
    in_specs = (
        P("row", ("sec", "col")),
        P(("sec", "col"), "row"),
        P(("sec", "col"), None),
        P(),
        P(),
    )
    out_specs = (P(("sec", "col"), "row"), P(("sec", "col"), None))
    return jax.shard_map(
        functools.partial(local, sizes), mesh=mesh, in_specs=in_specs, out_specs=out_specs, check_vma=False
    )
```

time: 250 us -> 121 us (0.48)
  waiting for transfers between devices: 203 us -> 0 us
  Pallas kernels: 0 us -> 110 us
  matrix products: 24 us -> 0 us
  between operations: 13.8 us -> 0.66 us
    pallas_call x0 -> x1, Pallas kernels: none -> 110 us  [exchange(): pl.pallas_call(functools.partial(kernel, sizes), out_shape=(jax.ShapeDtyp...]
    reduce_scatter x1 -> x0, waiting for transfers between devices: 85.2 us -> none  [local(): lax.psum_scatter(lax.dot_general(anc_rows, local_panel, (((0,), (1,)), ((...]
    psum x1 -> x0, waiting for transfers between devices: 69.7 us -> none  [local(): summed = lax.psum(update.reshape(local_rows, SW), 'row')]
    all_gather x1 -> x0, waiting for transfers between devices: 47.8 us -> none  [local(): anc_rows = lax.all_gather(anc_inverse, ('sec', 'col'), axis=1, tiled=True)]
    dot_general x2 -> x0, matrix products: 24 us -> none  [the longest x1 17.3 us: local(): lax.dot_general(anc_rows, local_panel, (((0,), (1,)), ((), ())), precisio...]
  transfers between devices with their start and end apart: 3 -> 0, of which waited for: 3 -> 0; matrix products, arithmetic and copies ran while one was open for 1% -> 0% of each run, Pallas kernels for 0% -> 0%
where the time goes in v1:
time: 121 us; the launch traced here: 120 us
  Pallas kernels  110 us (91%)
  other arithmetic  9.42 us (8%)
    pallas_call x1, Pallas kernels, exchange(): pl.pallas_call(functools.partial(kernel, sizes), out_shape=(jax.ShapeDtyp...  110 us
    mul x1, other arithmetic, local(): diag_block = (diag_inverse + update) * pair_mask.reshape(local_rows, SW)  4.71 us
    mul x1, other arithmetic, local(): panel.reshape(slot_count, SW, rows_here) * mask  3.15 us

profile of v1, /device:TPU:0, one launch (start us, length us, event | category | flops | bytes accessed | tf_op | source)
XLA Modules:
  0.0 119.9 jit_solution(14727749635960719690)
XLA Ops:
  0.6 0.7 dynamic-slice_multiply_fusion
  1.4 0.8 dynamic-slice_convert_fusion
  2.1 0.1 broadcast_bitcast_fusion
  2.2 0.1 compare_convert_fusion
  2.3 3.1 %fusion.2.panel_ref = f32[1024,512]{1,0:T(8,128)} fusion(f32[1024,512]{1,0:T(8,128)} %param.6, f32[2,512]{1,0:T(2,128)S(1)} %bitcast.20, f32[1024]{0:T(1024)S(1)} %bitcast.22), kind=kLoop, calls=%fused_computation.4 | loop fusion | flops 1048576 | bytes 4202496 | tf_op jit(solution)/shard_map/mul | solution.py:360
  5.4 0.0 copy-start
  5.4 109.7 %shard_map.68 = (f32[1024,512]{1,0:T(8,128)}, f32[1024,512]{1,0:T(8,128)}) custom-call(f32[512,256]{1,0:T(8,128)} %anc_ref.1, f32[1024,512]{1,0:T(8,128)} %fusion.2.panel_ref), custom_call_target="tpu_custom_call" | custom-call | tf_op jit(solution)/shard_map/pallas_call | solution.py:313
  115.2 0.0 copy-done
  115.2 4.7 %fusion = (f32[1024,512]{1,0:T(8,128)}, f32[1024,512]{1,0:T(8,128)}) fusion(f32[1024,512]{1,0:T(8,128)S(1)} %copy-done, f32[1024,512]{1,0:T(8,128)} %get-tuple-element.5, f32[2,512]{1,0:T(2,128)S(1)} %get-tuple-element.8, f32[1024]{0:T(1024)S(1)} %bitcast.23, f32[1024,512]{1,0:T(8,128)} %get-tuple-element.4, f32[2,512]{1,0:T(2,128)S(1)} %bitcast.21), kind=kLoop, calls=%fused_computation.1 | loop fusion | flops 3145728 | bytes 10498048 | tf_op jit(solution)/shard_map/mul | solution.py:364
  (2 shorter events, 0.0 us)
Async XLA Ops:
  5.4 109.8 %copy-start = (f32[1024,512]{1,0:T(8,128)S(1)}, f32[1024,512]{1,0:T(8,128)}, u32[]{:S(2)}) copy-start(f32[1024,512]{1,0:T(8,128)} %param.7) | copy-start | bytes 6291460

commit v2 on v1

--- a/solution.py
+++ b/solution.py
@@ -35,9 +35,9 @@
 
 def kernel(
     sizes,
-    anc_ref, panel_ref, prod_ref, upd_ref,
+    anc_ref, panel_ref, diag_ref, widths_ref, pattern_ref, prod_ref, upd_ref,
     anc, ah, al, ph, plo, pin, opp, oh, ol, qsend, qrecv, upack, urecv, usum, ugat,
-    zs, zr, ps, pr, os_, or_, qs, qr, us, ur, gs, gr,
+    zs, zr, ps, pr, os_, or_, qs, qr, us, ur, gs, gr, ds,
 ):
     nsec, nrow, ncol, nf, ns, nb, square = sizes
     rows, width = panel_ref.shape
@@ -64,6 +64,26 @@
             src_ref=src, dst_ref=dst, send_sem=send, recv_sem=recv, device_id=where, device_id_type=MESH
         )
 
+    first = (sec * ncol + col) * slots
+    blocks = width // B
+    fill = [widths_ref[first + j] for j in range(slots)]
+    load_diag = pltpu.make_async_copy(diag_ref, upd_ref, ds)
+
+    def inside(j, i):
+        return jnp.where(fill[j] > i, 1.0, 0.0).astype(F32)
+
+    def present(j, r, c):
+        return pattern_ref[first + j, r * blocks + c].astype(F32)
+
+    def keep(src, j, slot, r):
+        for i in range(wb):
+            here = pl.ds(j * SW + i * B, B)
+            for c in range(blocks):
+                cols = pl.ds(c * B, B)
+                high, low = split(src(i, cols) * (inside(j, i) * present(j, r, c)))
+                ph[slot, here, cols] = high
+                plo[slot, here, cols] = low
+
     has_left = (col > 0).astype(jnp.int32)
     has_right = (col < ncol - 1).astype(jnp.int32)
     barrier = pltpu.get_barrier_semaphore()
@@ -111,24 +131,27 @@
         ah[p] = high
         al[p] = low
 
-    @pl.when(col > 0)
+    def late(p):
+        return p // per == row
+
+    def send_mine():
+        pl.when(col > 0)(lambda: piece_copy(anc_ref, mine, 0).start())
+        pl.when(col < ncol - 1)(lambda: piece_copy(anc_ref, mine, 1).start())
+        piece_copy(anc_ref, mine, 2).start()
+
+    @pl.when(jnp.logical_not(late(mine)))
     def _():
-        piece_copy(anc_ref, mine, 0).start()
-
-    @pl.when(col < ncol - 1)
-    def _():
-        piece_copy(anc_ref, mine, 1).start()
-
-    piece_copy(anc_ref, mine, 2).start()
-    pass_on(anc_ref, mine)
+        send_mine()
+        pass_on(anc_ref, mine)
+
     for j in range(slots):
         for d in range(1, nf):
             panel_copy(d, j).start()
 
+    load_diag.start()
     halves(anc_ref, mine)
-    high, low = split(panel_ref[...])
-    ph[0] = high
-    plo[0] = low
+    for j in range(slots):
+        keep(lambda i, cols: panel_ref[pl.ds(j * SW + i * B, B), cols], j, 0, row)
 
     def from_left(t):
         p = mine - t
@@ -160,23 +183,31 @@
         halves(anc.at[p], p)
 
     other = (1 - sec) * ncol + col
-    from_partner(other)
-
-    def gather_step(t, carry):
-        pl.when(col - t >= 0)(lambda: from_left(t))
-        pl.when(col + t < ncol)(lambda: from_right(t))
-        pl.when(col - t >= 0)(lambda: from_partner(other - t))
-        pl.when(col + t < ncol)(lambda: from_partner(other + t))
-        return carry
-
-    lax.fori_loop(1, ncol, gather_step, 0)
+
+    def gather(phase):
+        def ready(p):
+            return late(p) if phase else jnp.logical_not(late(p))
+
+        pl.when(ready(other))(lambda: from_partner(other))
+
+        def step(t, carry):
+            left = col - t >= 0
+            right = col + t < ncol
+            pl.when(jnp.logical_and(left, ready(mine - t)))(lambda: from_left(t))
+            pl.when(jnp.logical_and(right, ready(mine + t)))(lambda: from_right(t))
+            pl.when(jnp.logical_and(left, ready(other - t)))(lambda: from_partner(other - t))
+            pl.when(jnp.logical_and(right, ready(other + t)))(lambda: from_partner(other + t))
+            return carry
+
+        lax.fori_loop(1, ncol, step, 0)
+
+    gather(0)
+    pl.when(late(mine))(send_mine)
 
     for j in range(slots):
         for d in range(1, nf):
             panel_copy(d, j).wait_recv()
-            high, low = split(pin[d - 1, j])
-            ph[d, pl.ds(j * SW, SW)] = high
-            plo[d, pl.ds(j * SW, SW)] = low
+            keep(lambda i, cols: pin[d - 1, j, pl.ds(i * B, B), cols], j, d, at((f + nf - d) % nf, s))
     for d in range(1, nf):
         for e in range(1, ns):
             for k in range(per):
@@ -208,16 +239,25 @@
             lax.fori_loop(0, SW // tm, target, 0)
             q_copy(e, j).start()
 
-    def own(i, carry):
+    def near(i, carry):
         rr = pl.ds(pl.multiple_of(i * tm, tm), tm)
-        for k in range(per):
-            p = at(f, s) * per + k
-            prod_ref[rr, pl.ds(k * pw, pw)] = dot3(ph[0, rr], plo[0, rr], ah[p], al[p], NN)
+        acc = jnp.zeros((tm, width), F32)
         for d in range(1, nf):
             for k in range(per):
                 p = at((f + nf - d) % nf, s) * per + k
                 cols = pl.ds(k * pw, pw)
-                prod_ref[rr] += dot3(ph[d, rr, cols], plo[d, rr, cols], ah[p], al[p], NT)
+                acc += dot3(ph[d, rr, cols], plo[d, rr, cols], ah[p], al[p], NT)
+        prod_ref[rr] = acc
+        return carry
+
+    lax.fori_loop(0, rows // tm, near, 0)
+    gather(1)
+
+    def own(i, carry):
+        rr = pl.ds(pl.multiple_of(i * tm, tm), tm)
+        for k in range(per):
+            p = row * per + k
+            prod_ref[rr, pl.ds(k * pw, pw)] += dot3(ph[0, rr], plo[0, rr], ah[p], al[p], NN)
         return carry
 
     lax.fori_loop(0, rows // tm, own, 0)
@@ -250,6 +290,13 @@
             u_copy(j, d).start()
 
     for j in range(slots):
+        for i in range(wb):
+            here = pl.ds(j * SW + i * B, B)
+            for c in range(blocks):
+                cols = pl.ds(c * B, B)
+                prod_ref[here, cols] = prod_ref[here, cols] * -(inside(j, i) * present(j, row, c))
+
+    for j in range(slots):
         for d in range(1, nrow):
             u_copy(j, d).wait_recv()
         total = upack[j, pl.ds(pl.multiple_of(row * part, 8), part)]
@@ -259,6 +306,7 @@
         for d in range(1, nrow):
             g_copy(j, d).start()
 
+    load_diag.wait()
     for j in range(slots):
         for d in range(1, nrow):
             u_copy(j, d).wait_send()
@@ -270,9 +318,12 @@
         for i in range(wb):
             for k in range(i, wb):
                 block = upack[j, pl.ds(spot * B, B)]
-                upd_ref[pl.ds(j * SW + i * B, B), pl.ds(k * B, B)] = block
+                held = inside(j, k)
+                upper = (pl.ds(j * SW + i * B, B), pl.ds(k * B, B))
+                upd_ref[upper] = (upd_ref[upper] + block) * held
                 if k > i:
-                    upd_ref[pl.ds(j * SW + k * B, B), pl.ds(i * B, B)] = block.T
+                    lower = (pl.ds(j * SW + k * B, B), pl.ds(i * B, B))
+                    upd_ref[lower] = (upd_ref[lower] + block.T) * held
                 spot += 1
 
     for j in range(slots):
@@ -297,7 +348,7 @@
     lax.fori_loop(0, ncol, drain, 0)
 
 
-def exchange(sizes, anc_inverse, panel):
+def local(sizes, anc_inverse, panel, diag_inverse, widths, pattern):
     nsec, nrow, ncol, nf, ns, nb, square = sizes
     rows, width = panel.shape
     pw = anc_inverse.shape[1]
@@ -310,10 +361,11 @@
     vm = pltpu.VMEM
     dma = pltpu.SemaphoreType.DMA
     whole = pl.BlockSpec(memory_space=pltpu.VMEM)
+    scalar = pl.BlockSpec(memory_space=pltpu.SMEM)
     return pl.pallas_call(
         functools.partial(kernel, sizes),
         out_shape=(jax.ShapeDtypeStruct((rows, width), F32), jax.ShapeDtypeStruct((rows, SW), F32)),
-        in_specs=[whole, whole],
+        in_specs=[whole, whole, pl.BlockSpec(memory_space=pl.ANY), scalar, scalar],
         out_specs=(whole, whole),
         scratch_shapes=[
             vm((pieces, width, pw), F32),
@@ -337,32 +389,12 @@
             dma((ns - 1, slots)), dma((ns - 1, slots)),
             dma((slots, nrow - 1)), dma((slots, nrow - 1)),
             dma((slots, nrow - 1)), dma((slots, nrow - 1)),
+            dma,
         ],
         compiler_params=pltpu.CompilerParams(
             collective_id=0, has_side_effects=True, vmem_limit_bytes=60 * 1024 * 1024
         ),
-    )(anc_inverse, panel)
-
-
-def local(sizes, anc_inverse, panel, diag_inverse, widths, pattern):
-    local_rows, rows_here = panel.shape
-    slot_count = local_rows // SW
-    slot_first = (lax.axis_index("sec") * lax.axis_size("col") + lax.axis_index("col")) * slot_count
-    blocks = rows_here // B
-    my_widths = lax.dynamic_slice_in_dim(widths, slot_first, slot_count)
-    my_pattern = lax.dynamic_slice(
-        pattern, (slot_first, lax.axis_index("row") * blocks), (slot_count, blocks)
-    )
-    block_mask = jnp.repeat(my_pattern.astype(F32), B, axis=1)
-    position = jnp.arange(SW, dtype=jnp.int32)
-    column_mask = (position[None, :] < my_widths[:, None] * B).astype(F32)
-    mask = column_mask[:, :, None] * block_mask[:, None, :]
-    masked = (panel.reshape(slot_count, SW, rows_here) * mask).reshape(local_rows, rows_here)
-    product, update = exchange(sizes, anc_inverse, masked)
-    product = product.reshape(slot_count, SW, rows_here) * mask
-    pair_mask = column_mask[:, :, None] * column_mask[:, None, :]
-    diag_block = (diag_inverse + update) * pair_mask.reshape(local_rows, SW)
-    return (-product.reshape(local_rows, rows_here), diag_block)
+    )(anc_inverse, panel, diag_inverse, widths, pattern)
 
 
 def solution(mesh):

time: 121 us -> 117 us (0.967)
  other arithmetic: 9.42 us -> 0 us
  local copies, waits for them, and re-layouts: 0.09 us -> 4.55 us
  Pallas kernels: 110 us -> 112 us
    mul x3 -> x0, other arithmetic: 8.59 us -> none  [the longest x1 4.71 us: local(): diag_block = (diag_inverse + update) * pair_mask.reshape(local_rows, SW)]
    unnamed x5 -> x4, local copies, waits for them, and re-layouts: 0.09 us -> 4.55 us
    pallas_call x1, Pallas kernels: 110 us -> 112 us  [local(): pl.pallas_call(functools.partial(kernel, sizes), out_shape=(jax.ShapeDtyp...]
where the time goes in v2:
time: 117 us
  Pallas kernels  112 us (96%)
  local copies, waits for them, and re-layouts  4.55 us (4%)
    pallas_call x1, Pallas kernels, local(): pl.pallas_call(functools.partial(kernel, sizes), out_shape=(jax.ShapeDtyp...  112 us
    unnamed x4, local copies, waits for them, and re-layouts  4.55 us

profile of v2, /device:TPU:0, one launch (start us, length us, event | category | flops | bytes accessed | tf_op | source)
XLA Modules:
  0.0 117.1 jit_solution(2226438329287774177)
XLA Ops:
  0.6 111.9 %shard_map.68 = (f32[1024,512]{1,0:T(8,128)}, f32[1024,512]{1,0:T(8,128)}) custom-call(f32[512,256]{1,0:T(8,128)} %anc_ref.1, f32[1024,512]{1,0:T(8,128)} %panel_ref.1, f32[1024,512]{1,0:T(8,128)} %diag_ref.1, s32[16]{0:T(128)} %widths_ref.1, s32[16,16]{1,0:T(8,128)} %pattern_ref.1), custom_call_target="tpu_custom_call" | custom-call | tf_op jit(solution)/shard_map/pallas_call | solution.py:365
  112.5 0.0 copy-start
  112.5 3.2 %copy.9 = f32[1024,512]{1,0:T(8,128)} copy(f32[1024,512]{1,0:T(8,128)} %get-tuple-element.4) | data formatting | bytes 4194304
  115.7 0.0 copy-done
  115.7 1.3 %copy.10 = f32[1024,512]{1,0:T(8,128)} copy(f32[1024,512]{1,0:T(8,128)S(1)} %copy-done) | data formatting | bytes 4194304
Async XLA Ops:
  112.5 3.2 %copy-start = (f32[1024,512]{1,0:T(8,128)S(1)}, f32[1024,512]{1,0:T(8,128)}, u32[]{:S(2)}) copy-start(f32[1024,512]{1,0:T(8,128)} %get-tuple-element.5) | copy-start | bytes 6291460

commit v3 on v2

--- a/solution.py
+++ b/solution.py
@@ -8,6 +8,7 @@
 
 B = 128
 SW = 512
+CHUNKS = 4
 F32 = jnp.float32
 BF = jnp.bfloat16
 MESH = pl.DeviceIdType.MESH
@@ -31,6 +32,23 @@
         if count % value == 0 and value * value <= count:
             low = value
     return count // low, low
+
+
+class Group:
+    def __init__(self, copies):
+        self.copies = copies
+
+    def start(self):
+        for one in self.copies:
+            one.start()
+
+    def wait_recv(self):
+        for one in self.copies:
+            one.wait_recv()
+
+    def wait_send(self):
+        for one in self.copies:
+            one.wait_send()
 
 
 def kernel(
@@ -105,7 +123,14 @@
 
     def piece_copy(src, p, way):
         where = ({"col": col - 1}, {"col": col + 1}, {"sec": 1 - sec})[way]
-        return copy(src, anc.at[p], zs.at[p, way], zr.at[p], where)
+        size = src.shape[0] // CHUNKS
+        return Group([
+            copy(
+                src.at[pl.ds(c * size, size)], anc.at[p, pl.ds(c * size, size)],
+                zs.at[p, way, c], zr.at[p, c], where,
+            )
+            for c in range(CHUNKS)
+        ])
 
     def opp_copy(src, d, e, k):
         return copy(
@@ -153,27 +178,12 @@
     for j in range(slots):
         keep(lambda i, cols: panel_ref[pl.ds(j * SW + i * B, B), cols], j, 0, row)
 
-    def from_left(t):
-        p = mine - t
-        piece_copy(anc_ref, p, 2).wait_recv()
-
-        @pl.when(col < ncol - 1)
-        def _():
-            piece_copy(anc.at[p], p, 1).start()
-
-        piece_copy(anc.at[p], p, 2).start()
-        pass_on(anc.at[p], p)
-        halves(anc.at[p], p)
-
-    def from_right(t):
-        p = mine + t
-        piece_copy(anc_ref, p, 2).wait_recv()
-
-        @pl.when(col > 0)
-        def _():
-            piece_copy(anc.at[p], p, 0).start()
-
-        piece_copy(anc.at[p], p, 2).start()
+    def relay(p, way, c, onward):
+        piece_copy(anc_ref, p, way).copies[c].wait_recv()
+        pl.when(onward)(lambda: piece_copy(anc.at[p], p, way).copies[c].start())
+        piece_copy(anc.at[p], p, 2).copies[c].start()
+
+    def settle(p):
         pass_on(anc.at[p], p)
         halves(anc.at[p], p)
 
@@ -188,17 +198,24 @@
         def ready(p):
             return late(p) if phase else jnp.logical_not(late(p))
 
-        pl.when(ready(other))(lambda: from_partner(other))
-
         def step(t, carry):
-            left = col - t >= 0
-            right = col + t < ncol
-            pl.when(jnp.logical_and(left, ready(mine - t)))(lambda: from_left(t))
-            pl.when(jnp.logical_and(right, ready(mine + t)))(lambda: from_right(t))
-            pl.when(jnp.logical_and(left, ready(other - t)))(lambda: from_partner(other - t))
-            pl.when(jnp.logical_and(right, ready(other + t)))(lambda: from_partner(other + t))
+            left = jnp.logical_and(col - t >= 0, ready(mine - t))
+            right = jnp.logical_and(col + t < ncol, ready(mine + t))
+            for c in range(CHUNKS):
+                pl.when(left)(lambda: relay(mine - t, 1, c, col < ncol - 1))
+                pl.when(right)(lambda: relay(mine + t, 0, c, col > 0))
+            pl.when(left)(lambda: settle(mine - t))
+            pl.when(right)(lambda: settle(mine + t))
+            partners(t)
             return carry
 
+        def partners(t):
+            left = jnp.logical_and(col - t >= 0, ready(other - t))
+            right = jnp.logical_and(col + t < ncol, ready(other + t))
+            pl.when(left)(lambda: from_partner(other - t))
+            pl.when(jnp.logical_and(right, t > 0))(lambda: from_partner(other + t))
+
+        partners(0)
         lax.fori_loop(1, ncol, step, 0)
 
     gather(0)
@@ -383,7 +400,7 @@
             vm((slots, nrow - 1, part, B), F32),
             vm((slots, part, B), F32),
             vm((slots, nrow - 1, part, B), F32),
-            dma((pieces, 3)), dma((pieces,)),
+            dma((pieces, 3, CHUNKS)), dma((pieces, CHUNKS)),
             dma((nf - 1, slots)), dma((nf - 1, slots)),
             dma((nf - 1, ns - 1, per)), dma((nf - 1, ns - 1, per)),
             dma((ns - 1, slots)), dma((ns - 1, slots)),

time: 117 us -> 116 us (level)
  the two profiles are of different devices: /device:TPU:0 before, /device:TPU:31 now
where the time goes in v3:
time: 116 us
  Pallas kernels  110 us (95%)
  local copies, waits for them, and re-layouts  4.55 us (4%)
    pallas_call x1, Pallas kernels, local(): pl.pallas_call(functools.partial(kernel, sizes), out_shape=(jax.ShapeDtyp...  110 us
    unnamed x4, local copies, waits for them, and re-layouts  4.55 us

profile of v3, /device:TPU:31, one launch (start us, length us, event | category | flops | bytes accessed | tf_op | source)
XLA Modules:
  0.0 115.7 jit_solution(5734699985401372545)
XLA Ops:
  0.6 110.5 %shard_map.68 = (f32[1024,512]{1,0:T(8,128)}, f32[1024,512]{1,0:T(8,128)}) custom-call(f32[512,256]{1,0:T(8,128)} %anc_ref.1, f32[1024,512]{1,0:T(8,128)} %panel_ref.1, f32[1024,512]{1,0:T(8,128)} %diag_ref.1, s32[16]{0:T(128)} %widths_ref.1, s32[16,16]{1,0:T(8,128)} %pattern_ref.1), custom_call_target="tpu_custom_call" | custom-call | tf_op jit(solution)/shard_map/pallas_call | solution.py:382
  111.1 0.0 copy-start
  111.1 3.2 %copy.9 = f32[1024,512]{1,0:T(8,128)} copy(f32[1024,512]{1,0:T(8,128)} %get-tuple-element.4) | data formatting | bytes 4194304
  114.4 0.0 copy-done
  114.4 1.3 %copy.10 = f32[1024,512]{1,0:T(8,128)} copy(f32[1024,512]{1,0:T(8,128)S(1)} %copy-done) | data formatting | bytes 4194304
Async XLA Ops:
  111.1 3.2 %copy-start = (f32[1024,512]{1,0:T(8,128)S(1)}, f32[1024,512]{1,0:T(8,128)}, u32[]{:S(2)}) copy-start(f32[1024,512]{1,0:T(8,128)} %get-tuple-element.5) | copy-start | bytes 6291460

commit v4 on v3

--- a/solution.py
+++ b/solution.py
@@ -8,7 +8,7 @@
 
 B = 128
 SW = 512
-CHUNKS = 4
+CHUNKS = 8
 F32 = jnp.float32
 BF = jnp.bfloat16
 MESH = pl.DeviceIdType.MESH

time: 116 us -> 114 us (0.983)
  the two profiles are of different devices: /device:TPU:31 before, /device:TPU:0 now
where the time goes in v4:
time: 114 us; the launch traced here: 112 us
  Pallas kernels  107 us (94%)
  local copies, waits for them, and re-layouts  4.55 us (4%)
    pallas_call x1, Pallas kernels, local(): pl.pallas_call(functools.partial(kernel, sizes), out_shape=(jax.ShapeDtyp...  107 us
    unnamed x4, local copies, waits for them, and re-layouts  4.55 us

profile of v4, /device:TPU:0, one launch (start us, length us, event | category | flops | bytes accessed | tf_op | source)
XLA Modules:
  0.0 111.9 jit_solution(6568552032882061422)
XLA Ops:
  0.6 106.7 %shard_map.68 = (f32[1024,512]{1,0:T(8,128)}, f32[1024,512]{1,0:T(8,128)}) custom-call(f32[512,256]{1,0:T(8,128)} %anc_ref.1, f32[1024,512]{1,0:T(8,128)} %panel_ref.1, f32[1024,512]{1,0:T(8,128)} %diag_ref.1, s32[16]{0:T(128)} %widths_ref.1, s32[16,16]{1,0:T(8,128)} %pattern_ref.1), custom_call_target="tpu_custom_call" | custom-call | tf_op jit(solution)/shard_map/pallas_call | solution.py:382
  107.4 0.0 copy-start
  107.4 3.2 %copy.9 = f32[1024,512]{1,0:T(8,128)} copy(f32[1024,512]{1,0:T(8,128)} %get-tuple-element.4) | data formatting | bytes 4194304
  110.6 0.0 copy-done
  110.6 1.3 %copy.10 = f32[1024,512]{1,0:T(8,128)} copy(f32[1024,512]{1,0:T(8,128)S(1)} %copy-done) | data formatting | bytes 4194304
Async XLA Ops:
  107.4 3.2 %copy-start = (f32[1024,512]{1,0:T(8,128)S(1)}, f32[1024,512]{1,0:T(8,128)}, u32[]{:S(2)}) copy-start(f32[1024,512]{1,0:T(8,128)} %get-tuple-element.5) | copy-start | bytes 6291460
